TPU v7x, 512 devices: a whole 4x8x8 slice. The times are simulated.
512 devices in a mesh: lang: 16 (over z_lo, y), bulk: 32 (over z_hi, x, core).
Axes of the slice: x: 4, y: 8, z: 8 (z_hi: 4, z_lo: 2; z = z_hi * 2 + z_lo), core: 2. Of those that a mesh axis runs over, the one named last changes fastest.
Arguments:
- sources: bfloat16 [524288, 1024], P(('lang', 'bulk')), may hold values from -24 to 24
- lang_ids: int32 [4096], P(('lang', 'bulk')), may hold values from 0 to 15
- centers: float32 [16, 1024], replicated, may hold values from -3 to 3
- targets: bfloat16 [1024, 1024], P('bulk'), may hold values from -12 to 12
Outputs:
- hubness: float32 [1024], P('bulk')
- source_logsum: float32 [524288], P(('lang', 'bulk'))
- source_match: float32 [524288], P(('lang', 'bulk'))
All inputs are finite; a program needn't handle non-finite values.
Results may differ from a plain program's by a relative error of at most 0.0043.
Values may be sent and summed in bfloat16 or wider, within the bound.
A program may use at most 64 MiB of HBM per device.

v0:
```python
import jax
import jax.numpy as jnp
from jax import lax
from jax.sharding import PartitionSpec as P


def tile_scores(target_piece, centered, temper):
    products = lax.dot_general(
        target_piece, centered, (((1,), (1,)), ((), ())), preferred_element_type=jnp.float32
    )
    return products * temper


def read_update(carried, score_tile, hub_part):
    run_peak, run_weight, run_match = carried
    adjusted = 2.0 * score_tile - hub_part[:, None]
    new_peak = jnp.max(adjusted, axis=0)
    weights = jnp.exp(adjusted - new_peak[None, :])
    factor = jnp.exp(run_peak - new_peak)
    return (
        new_peak,
        run_weight * factor + jnp.sum(weights, axis=0),
        run_match * factor + jnp.sum(weights * score_tile, axis=0),
    )


def per_device(sources, lang_ids, centers, targets):
    source_count, feature_width = sources.shape
    block_count = lang_ids.shape[0]
    lang_count = centers.shape[0]
    temper = feature_width ** (-0.5)
    target_local = targets.shape[0]
    chosen = (lang_ids[:, None] == jnp.arange(lang_count, dtype=jnp.int32)[None, :]).astype(
        jnp.float32
    )
    offsets = jnp.dot(
        chosen, centers, precision=lax.Precision.HIGHEST, preferred_element_type=jnp.float32
    )
    grouped = sources.astype(jnp.float32).reshape(
        block_count, source_count // block_count, feature_width
    )
    centered = (
        (grouped - offsets[:, None, :]).reshape(source_count, feature_width).astype(jnp.bfloat16)
    )
    score_tile = tile_scores(lax.all_gather(targets, "bulk", axis=0, tiled=True), centered, temper)
    tile_peak = jnp.max(score_tile, axis=1)
    tile_weight = jnp.sum(jnp.exp(score_tile - tile_peak[:, None]), axis=1)
    score_tile, tile_peak, tile_weight = (score_tile, tile_peak, tile_weight)
    global_peak = lax.pmax(tile_peak, ("lang", "bulk"))
    global_weight = lax.psum(tile_weight * jnp.exp(tile_peak - global_peak), ("lang", "bulk"))
    hubness = global_peak + jnp.log(global_weight)
    start_state = (
        jnp.full((source_count,), -jnp.inf, jnp.float32),
        jnp.zeros((source_count,), jnp.float32),
        jnp.zeros((source_count,), jnp.float32),
    )
    score_tile = tile_scores(lax.all_gather(targets, "bulk", axis=0, tiled=True), centered, temper)
    final_state = read_update(start_state, score_tile, hubness)
    source_logsum = final_state[0] + jnp.log(final_state[1])
    source_match = final_state[2] / final_state[1]
    own_hub = lax.dynamic_slice_in_dim(hubness, lax.axis_index("bulk") * target_local, target_local)
    return (own_hub, source_logsum, source_match)


def solution(mesh):
    in_specs = (P(("lang", "bulk"), None), P(("lang", "bulk")), P(), P("bulk", None))
    out_specs = (P("bulk"), P(("lang", "bulk")), P(("lang", "bulk")))
    return jax.shard_map(
        per_device, mesh=mesh, in_specs=in_specs, out_specs=out_specs, check_vma=False
    )
```

profile of v0, /device:TPU:1, one launch (start us, length us, event | category | flops | bytes accessed | tf_op | source)
XLA Modules:
  0.0 289.6 jit_solution(16624731422087546585)
XLA Ops:
  7.2 0.0 copy-start
  7.2 0.0 all-gather.2.cloned.1.call-start
  7.2 0.7 all-gather.2.cloned.1.call-update
  7.9 0.1 copy-done
  8.0 0.9 fusion.3
  8.9 2.1 fusion
  11.0 66.6 %all-gather.2.cloned.1.call-done = bf16[1024,1024]{1,0:T(8,128)(2,1)} async-done(((bf16[32,1024]{1,0:T(8,128)(2,1)}), bf16[1024,1024]{1,0:T(8,128)(2,1)}) %all-gather.2.cloned.1.call-update) | async-done | bytes 2097168 | tf_op jit(solution)/shard_map/all_gather | solution.py:45
  77.6 5.9 %multiply_reduce_fusion.1 = (f32[1024]{0:T(1024)S(1)}, f32[1024,1024]{0,1:T(8,128)}) fusion(bf16[1024,1024]{1,0:T(8,128)(2,1)S(1)} %fusion, bf16[1024,1024]{1,0:T(8,128)(2,1)} %all-gather.2.cloned.1.call-done), kind=kOutput, calls=%fused_computation.7 | convolution fusion | flops 2149579776 | bytes 8392704 | tf_op jit(solution)/shard_map/dot_general | solution.py:8
  83.5 95.8 %pmax.7 = f32[1024]{0:T(1024)S(1)} all-reduce(f32[1024]{0:T(1024)S(1)} %get-tuple-element.7), channel_id=1, replica_groups=mesh['lang'=16,'bulk'=32] {'lang','bulk'}, use_global_device_ids=true, to_apply=%region_1.0 | all-reduce | flops 1024 | bytes 8192 | tf_op jit(solution)/shard_map/pmax | solution.py:49
  179.3 3.1 %exponential_reduce_fusion = f32[1024]{0:T(1024)S(1)} fusion(f32[1024,1024]{0,1:T(8,128)} %get-tuple-element.8, f32[1024]{0:T(1024)S(1)} %get-tuple-element.7), kind=kLoop, calls=%fused_computation.2 | loop fusion | flops 3144704 | bytes 4202496 | tf_op jit(solution)/shard_map/reduce_sum | solution.py:47
  182.4 94.4 %psum.7 = f32[1024]{0:T(1024)S(1)} all-reduce(f32[1024]{0:T(1024)S(1)} %exponential_multiply_fusion.1), channel_id=1, replica_groups=mesh['lang'=16,'bulk'=32] {'lang','bulk'}, use_global_device_ids=true, to_apply=%region_3.0 | all-reduce | flops 1024 | bytes 8192 | tf_op jit(solution)/shard_map/psum | solution.py:50
  276.8 0.0 copy-start.1
  276.8 2.8 fusion.1
  279.6 0.6 copy-done.1
  280.2 1.3 multiply_reduce_fusion
  281.5 0.6 dynamic_slice.3
  282.1 0.6 add_divide_fusion
  (2 shorter events, 0.0 us)
Async XLA Ops:
  7.2 0.8 copy-start
  7.2 70.4 %all-gather.2.cloned.1.call-start = ((), (), s32[]{:S(2)}) async-start(), calls=%async_computation | async-start | bytes 2162688 | tf_op jit(solution)/shard_map/all_gather | solution.py:45
  276.8 3.4 %copy-start.1 = (f32[1024,1024]{0,1:T(8,128)S(1)}, f32[1024,1024]{0,1:T(8,128)}, u32[]{:S(2)}) copy-start(f32[1024,1024]{0,1:T(8,128)} %get-tuple-element.8) | copy-start | bytes 12582916
Sparse Core Ops, SparseCore 0:
  11.1 66.4 all-gather.1
where the time goes:
time: 290 us
  blocking collectives  190 us (66%)
  waiting for transfers between devices  67.3 us (23%)
  between operations  14.1 us (5%)
  other arithmetic  9.93 us (3%)
  matrix products  6.74 us (2%)
    pmax x1, blocking collectives, per_device(): global_peak = lax.pmax(tile_peak, ('lang', 'bulk'))  95.8 us
    psum x1, blocking collectives, per_device(): lax.psum(tile_weight * jnp.exp(tile_peak - global_peak), ('lang', 'bulk'))  94.4 us
    all_gather x1, waiting for transfers between devices, per_device(): lax.all_gather(targets, 'bulk', axis=0, tiled=True)  66.6 us
    dot_general x1, matrix products, tile_scores(): lax.dot_general(target_piece, centered, (((1,), (1,)), ((), ())), preferr...  5.89 us
  transfers between devices with their start and end apart: 1, of which 1 were waited for; matrix products, arithmetic and copies ran while one was open for 1% of the time, Pallas kernels for 0%

commit v1 on v0

v1 whole, which is shorter than its diff:
```python
import functools

import jax
import jax.numpy as jnp
from jax import lax
from jax.experimental import pallas as pl
from jax.experimental.pallas import tpu as pltpu
from jax.sharding import PartitionSpec as P

MESH = pl.DeviceIdType.MESH
SENDS = (4, 3, 5, 2, 6, 1, 7)


def kernel(
    rowblk,
    ids_ref, centers_ref, targets_ref, sources_ref,
    hub_ref, logsum_ref, match_ref,
    raw, centered, held, scores, hubs, parts,
    load_sem,
    z_send, z_recv, x_send, x_recv, c_send, c_recv,
    r_send, r_recv,
):
    lang = lax.axis_index("lang")
    bulk = lax.axis_index("bulk")
    zl, y = lang // 8, lang % 8
    k, x, c = bulk // 8, (bulk // 2) % 4, bulk % 2
    low = bulk % 8
    z = k * 2 + zl
    width = centers_ref.shape[1]
    temper = width ** (-0.5)
    nblk = raw.shape[0]
    piece_rows = targets_ref.shape[0]
    half = piece_rows // 2

    def at_bulk(kk, xx, cc):
        return (lang, kk * 8 + xx * 2 + cc)

    def slot(dk, dx, cc):
        return cc * 16 + lax.rem(k + dk, 4) * 4 + lax.rem(x + dx, 4)

    up_k = at_bulk(lax.rem(k + 1, 4), x, c)
    down_k = at_bulk(lax.rem(k + 3, 4), x, c)
    up_x = at_bulk(k, lax.rem(x + 1, 4), c)
    down_x = at_bulk(k, lax.rem(x + 3, 4), c)
    sibling = at_bulk(k, x, 1 - c)

    stage_me = (low, y, z)
    stage_peer = (
        lambda j: (lang, k * 8 + lax.rem(low + j, 8)),
        lambda j: (zl * 8 + lax.rem(y + j, 8), bulk),
        lambda j: (lax.rem(z + j, 2) * 8 + y, (lax.rem(z + j, 8) // 2) * 8 + low),
    )

    loads = []
    for b in range(nblk):
        load = pltpu.make_async_copy(
            sources_ref.at[pl.ds(b * rowblk, rowblk), :], raw.at[b], load_sem.at[b]
        )
        load.start()
        loads.append(load)

    barrier = pltpu.get_barrier_semaphore()
    for stage in range(3):
        for j in range(1, 8):
            pl.semaphore_signal(
                barrier, inc=1, device_id=stage_peer[stage](j), device_id_type=MESH
            )
    pl.semaphore_wait(barrier, 21)

    started = []

    def send(src, dst, send_sem, recv_sem, device):
        copy = pltpu.make_async_remote_copy(
            src_ref=src, dst_ref=dst, send_sem=send_sem, recv_sem=recv_sem,
            device_id=device, device_id_type=MESH,
        )
        copy.start()
        started.append(copy)

    def arrived(dst, send_sem, recv_sem):
        pltpu.make_async_remote_copy(
            src_ref=dst, dst_ref=dst, send_sem=send_sem, recv_sem=recv_sem,
            device_id=sibling, device_id_type=MESH,
        ).wait_recv()

    def piece(dk, dx):
        return held.at[slot(dk, dx, c)]

    def part(ref, which):
        return ref.at[pl.ds(which * half, half), :]

    def to_sibling(dk, dx, src=None):
        dst = piece(dk, dx)
        send(dst if src is None else src, dst, c_send.at[dk, dx], c_recv.at[dk, dx], sibling)

    def along_x(dk, src=None):
        dst = piece(dk, 0)
        src = dst if src is None else src
        send(src, dst, x_send.at[dk, 0], x_recv.at[dk, 0], up_x)
        send(src, dst, x_send.at[dk, 1], x_recv.at[dk, 1], down_x)
        to_sibling(dk, 0, src)

    def relay_x(dk):
        left = piece(dk, 3)
        arrived(left, x_send.at[dk, 0], x_recv.at[dk, 0])
        send(part(left, 0), part(left, 0), x_send.at[dk, 2], x_recv.at[dk, 2], up_x)
        to_sibling(dk, 3)
        right = piece(dk, 1)
        arrived(right, x_send.at[dk, 1], x_recv.at[dk, 1])
        send(part(right, 1), part(right, 1), x_send.at[dk, 3], x_recv.at[dk, 3], down_x)
        to_sibling(dk, 1)

    def finish_x(dk):
        far = piece(dk, 2)
        arrived(part(far, 0), x_send.at[dk, 2], x_recv.at[dk, 2])
        arrived(part(far, 1), x_send.at[dk, 3], x_recv.at[dk, 3])
        to_sibling(dk, 2)

    own = piece(0, 0)
    send(targets_ref, own, z_send.at[0], z_recv.at[0], up_k)
    send(targets_ref, own, z_send.at[1], z_recv.at[1], down_k)
    along_x(0, targets_ref)
    held[slot(0, 0, c)] = targets_ref[...]

    for b in range(nblk):
        loads[b].wait()
        offset = centers_ref[pl.ds(ids_ref[b], 1), :]
        centered[b] = (raw[b].astype(jnp.float32) - offset).astype(jnp.bfloat16)

    below = piece(3, 0)
    arrived(below, z_send.at[0], z_recv.at[0])
    send(part(below, 0), part(below, 0), z_send.at[2], z_recv.at[2], up_k)
    along_x(3)
    above = piece(1, 0)
    arrived(above, z_send.at[1], z_recv.at[1])
    send(part(above, 1), part(above, 1), z_send.at[3], z_recv.at[3], down_k)
    along_x(1)
    relay_x(0)
    relay_x(3)
    relay_x(1)
    across = piece(2, 0)
    arrived(part(across, 0), z_send.at[2], z_recv.at[2])
    arrived(part(across, 1), z_send.at[3], z_recv.at[3])
    along_x(2)
    finish_x(0)
    relay_x(2)
    finish_x(3)
    finish_x(1)
    finish_x(2)
    for dk in range(4):
        for dx in range(4):
            arrived(held.at[slot(dk, dx, 1 - c)], c_send.at[dk, dx], c_recv.at[dk, dx])

    count = held.shape[0] * piece_rows

    def score_step(b, carried):
        peak, weight = carried
        tile = lax.dot_general(
            centered[b], held[...].reshape(count, width), (((1,), (1,)), ((), ())),
            preferred_element_type=jnp.float32,
        ) * temper
        scores[b] = tile
        grouped = tile.reshape(rowblk // 8, 8, count)
        new_peak = jnp.maximum(peak, jnp.max(grouped, axis=0))
        weight = weight * jnp.exp(peak - new_peak) + jnp.sum(
            jnp.exp(grouped - new_peak[None]), axis=0
        )
        return new_peak, weight

    peak, weight = lax.fori_loop(
        0, nblk, score_step,
        (jnp.full((8, count), -jnp.inf, jnp.float32), jnp.zeros((8, count), jnp.float32)),
    )
    top = jnp.max(peak, axis=0, keepdims=True)
    hub = top + jnp.log(jnp.sum(weight * jnp.exp(peak - top), axis=0, keepdims=True))
    for j in range(8):
        hubs[0, pl.ds(j, 1), :] = hub[:, j * 128:(j + 1) * 128]

    for stage in range(3):
        me = stage_me[stage]
        for j in SENDS:
            send(
                hubs.at[stage], parts.at[stage, me], r_send.at[stage, j], r_recv.at[stage, j],
                stage_peer[stage](j),
            )
        parts[stage, me] = hubs[stage]
        for j in range(1, 8):
            arrived(
                parts.at[stage, lax.rem(me + 8 - j, 8)], r_send.at[stage, j], r_recv.at[stage, j]
            )
        every = parts[stage]
        most = jnp.max(every, axis=0)
        hubs[stage + 1] = most + jnp.log(jnp.sum(jnp.exp(every - most[None]), axis=0))

    hub_row = jnp.concatenate([hubs[3, pl.ds(j, 1), :] for j in range(8)], axis=1)
    where_own = slot(0, 0, c)
    lanes = hubs[3, pl.ds(where_own // 4, 1), :]
    quarter = where_own % 4
    mine = jnp.zeros((1, piece_rows), jnp.float32)
    for q in range(4):
        mine = jnp.where(quarter == q, lanes[:, q * piece_rows:(q + 1) * piece_rows], mine)
    hub_ref[...] = mine

    eye = lax.broadcasted_iota(jnp.int32, (rowblk, rowblk), 0) == lax.broadcasted_iota(
        jnp.int32, (rowblk, rowblk), 1
    )

    def read_step(b, unused):
        tile = scores[b]
        adjusted = 2.0 * tile - hub_row
        most = jnp.max(adjusted, axis=1, keepdims=True)
        weights = jnp.exp(adjusted - most)
        summed = jnp.sum(weights, axis=1, keepdims=True)
        matched = jnp.sum(weights * tile, axis=1, keepdims=True)
        logsum = most + jnp.log(summed)
        match = matched / summed
        logsum_ref[pl.ds(b, 1), :] = jnp.sum(jnp.where(eye, logsum, 0.0), axis=0, keepdims=True)
        match_ref[pl.ds(b, 1), :] = jnp.sum(jnp.where(eye, match, 0.0), axis=0, keepdims=True)
        return unused

    lax.fori_loop(0, nblk, read_step, 0)
    for copy in started:
        copy.wait_send()


def per_device(sources, lang_ids, centers, targets):
    rows, width = sources.shape
    nblk = lang_ids.shape[0]
    rowblk = rows // nblk
    piece_rows = targets.shape[0]
    count = 32 * piece_rows
    vmem = pl.BlockSpec(memory_space=pltpu.VMEM)
    dma = pltpu.SemaphoreType.DMA
    hub, logsum, match = pl.pallas_call(
        functools.partial(kernel, rowblk),
        out_shape=(
            jax.ShapeDtypeStruct((1, piece_rows), jnp.float32),
            jax.ShapeDtypeStruct((nblk, rowblk), jnp.float32),
            jax.ShapeDtypeStruct((nblk, rowblk), jnp.float32),
        ),
        in_specs=[
            pl.BlockSpec(memory_space=pltpu.SMEM), vmem, vmem,
            pl.BlockSpec(memory_space=pl.ANY),
        ],
        out_specs=(vmem, vmem, vmem),
        scratch_shapes=[
            pltpu.VMEM((nblk, rowblk, width), jnp.bfloat16),
            pltpu.VMEM((nblk, rowblk, width), jnp.bfloat16),
            pltpu.VMEM((32, piece_rows, width), jnp.bfloat16),
            pltpu.VMEM((nblk, rowblk, count), jnp.float32),
            pltpu.VMEM((4, 8, count // 8), jnp.float32),
            pltpu.VMEM((3, 8, 8, count // 8), jnp.float32),
            dma((nblk,)),
            dma((4,)), dma((4,)),
            dma((4, 4)), dma((4, 4)),
            dma((4, 4)), dma((4, 4)),
            dma((3, 8)), dma((3, 8)),
        ],
        compiler_params=pltpu.CompilerParams(
            collective_id=0, has_side_effects=True, vmem_limit_bytes=48 * 1024 * 1024
        ),
        name="csls",
    )(lang_ids, centers, targets, sources)
    return hub.reshape(piece_rows), logsum.reshape(rows), match.reshape(rows)


def solution(mesh):
    in_specs = (P(("lang", "bulk"), None), P(("lang", "bulk")), P(), P("bulk", None))
    out_specs = (P("bulk"), P(("lang", "bulk")), P(("lang", "bulk")))
    return jax.shard_map(
        per_device, mesh=mesh, in_specs=in_specs, out_specs=out_specs, check_vma=False
    )
```

time: 290 us -> 63.7 us (0.22)
  blocking collectives: 190 us -> 0 us
  waiting for transfers between devices: 67.3 us -> 0 us
  Pallas kernels: 0 us -> 57.1 us
  between operations: 14.1 us -> 0.65 us
  other arithmetic: 9.93 us -> 0 us
  matrix products: 6.74 us -> 0 us
  local copies, waits for them, and re-layouts: 1.31 us -> 5.62 us
    pmax x1 -> x0, blocking collectives: 95.8 us -> none  [per_device(): global_peak = lax.pmax(tile_peak, ('lang', 'bulk'))]
    psum x1 -> x0, blocking collectives: 94.4 us -> none  [per_device(): lax.psum(tile_weight * jnp.exp(tile_peak - global_peak), ('lang', 'bulk'))]
    all_gather x1 -> x0, waiting for transfers between devices: 66.6 us -> none  [per_device(): lax.all_gather(targets, 'bulk', axis=0, tiled=True)]
    pallas_call x0 -> x1, Pallas kernels: none -> 57.1 us  [per_device(): pl.pallas_call(functools.partial(kernel, rowblk), out_shape=(jax.ShapeDty...]
    dot_general x2 -> x0, matrix products: 6.74 us -> none  [the longest x1 5.89 us: tile_scores(): lax.dot_general(target_piece, centered, (((1,), (1,)), ((), ())), preferr...]
    unnamed x4 -> x11, local copies, waits for them, and re-layouts: 0.72 us -> 5.62 us
    reduce_sum x2 -> x0, other arithmetic: 4.35 us -> none  [the longest x1 3.05 us: per_device(): tile_weight = jnp.sum(jnp.exp(score_tile - tile_peak[:, None]), axis=1)]
  transfers between devices with their start and end apart: 1 -> 0, of which waited for: 1 -> 0; matrix products, arithmetic and copies ran while one was open for 1% -> 0% of each run, Pallas kernels for 0% -> 0%
where the time goes in v1:
time: 63.7 us; the launch traced here: 63.3 us
  Pallas kernels  57.1 us (90%)
  local copies, waits for them, and re-layouts  5.62 us (9%)
  between operations  0.65 us (1%)
    pallas_call x1, Pallas kernels, per_device(): pl.pallas_call(functools.partial(kernel, rowblk), out_shape=(jax.ShapeDty...  57.1 us
    unnamed x11, local copies, waits for them, and re-layouts  5.62 us

profile of v1, /device:TPU:1, one launch (start us, length us, event | category | flops | bytes accessed | tf_op | source)
XLA Modules:
  0.0 63.3 jit_solution(13005653529756512065)
XLA Ops:
  0.6 0.0 copy-start
  0.6 1.6 %copy-done = bf16[1024,1024]{1,0:T(8,128)(2,1)S(1)} copy-done((bf16[1024,1024]{1,0:T(8,128)(2,1)S(1)}, bf16[1024,1024]{1,0:T(8,128)(2,1)}, u32[]{:S(2)}) %copy-start) | copy-done | bytes 2097176
  2.2 0.0 copy-start.1
  2.2 0.8 %copy-done.1 = f32[16,1024]{1,0:T(8,128)S(1)} copy-done((f32[16,1024]{1,0:T(8,128)S(1)}, f32[16,1024]{1,0:T(8,128)}, u32[]{:S(2)}) %copy-start.1) | copy-done | bytes 65560
  3.1 0.0 copy-start.2
  3.1 0.8 %copy-done.2 = bf16[32,1024]{1,0:T(8,128)(2,1)S(1)} copy-done((bf16[32,1024]{1,0:T(8,128)(2,1)S(1)}, bf16[32,1024]{1,0:T(8,128)(2,1)}, u32[]{:S(2)}) %copy-start.2) | copy-done | bytes 65560
  3.9 0.0 copy-start.3
  3.9 0.7 %copy-done.3 = s32[8]{0:T(128)S(1)} copy-done((s32[8]{0:T(128)S(1)}, s32[8]{0:T(128)}, u32[]{:S(2)}) %copy-start.3) | copy-done | bytes 56
  4.6 57.1 %csls.1 = (f32[1,32]{1,0:T(1,128)S(1)}, f32[8,128]{1,0:T(8,128)S(1)}, f32[8,128]{1,0:T(8,128)S(1)}) custom-call(s32[8]{0:T(128)S(1)} %copy-done.3, f32[16,1024]{1,0:T(8,128)S(1)} %copy-done.1, bf16[32,1024]{1,0:T(8,128)(2,1)S(1)} %copy-done.2, bf16[1024,1024]{1,0:T(8,128)(2,1)S(1)} %copy-done), custom_call_target="tpu_custom_call" | custom-call | tf_op jit(solution)/shard_map/csls/pallas_call | solution.py:234
  61.6 0.5 copy.10
  62.1 0.6 copy.11
  62.7 0.6 copy.12
Async XLA Ops:
  0.6 1.6 %copy-start = (bf16[1024,1024]{1,0:T(8,128)(2,1)S(1)}, bf16[1024,1024]{1,0:T(8,128)(2,1)}, u32[]{:S(2)}) copy-start(bf16[1024,1024]{1,0:T(8,128)(2,1)} %sources_ref.1) | copy-start | bytes 6291460
  2.2 0.8 %copy-start.1 = (f32[16,1024]{1,0:T(8,128)S(1)}, f32[16,1024]{1,0:T(8,128)}, u32[]{:S(2)}) copy-start(f32[16,1024]{1,0:T(8,128)} %centers_ref.1) | copy-start | bytes 196612
  3.1 0.8 %copy-start.2 = (bf16[32,1024]{1,0:T(8,128)(2,1)S(1)}, bf16[32,1024]{1,0:T(8,128)(2,1)}, u32[]{:S(2)}) copy-start(bf16[32,1024]{1,0:T(8,128)(2,1)} %targets_ref.1) | copy-start | bytes 196612
  3.9 0.7 %copy-start.3 = (s32[8]{0:T(128)S(1)}, s32[8]{0:T(128)}, u32[]{:S(2)}) copy-start(s32[8]{0:T(128)} %ids_ref.1) | copy-start | bytes 100

commit v2 on v1

v2 whole, which is shorter than its diff:
```python
import functools

import jax
import jax.numpy as jnp
from jax import lax
from jax.experimental import pallas as pl
from jax.experimental.pallas import tpu as pltpu
from jax.sharding import PartitionSpec as P

MESH = pl.DeviceIdType.MESH
SENDS = (4, 3, 5, 2, 6, 1, 7)
FAR_DIRECT = (0, 1, 2, 3)


def kernel(
    rowblk,
    ids_hbm, centers_hbm, targets_hbm, sources_hbm,
    hub_ref, logsum_ref, match_ref,
    ids, centers, raw, centered, held, scores, hubs, parts,
    load_sem, small_sem,
    z_send, z_recv, x_send, x_recv, y_send, y_recv, c_send, c_recv,
    r_send, r_recv,
):
    lang = lax.axis_index("lang")
    bulk = lax.axis_index("bulk")
    zl, y = lang // 8, lang % 8
    k, x, c = bulk // 8, (bulk // 2) % 4, bulk % 2
    low = bulk % 8
    z = k * 2 + zl
    nblk, _, width = raw.shape
    temper = width ** (-0.5)
    piece_rows = held.shape[1]
    half = piece_rows // 2
    group = 8 * piece_rows
    mine = y % 2

    def at_bulk(kk, xx, cc):
        return (lang, kk * 8 + xx * 2 + cc)

    def slot(dk, dx, cc):
        return lax.rem(k + dk, 4) * 8 + lax.rem(x + dx, 4) * 2 + cc

    up_k = at_bulk(lax.rem(k + 1, 4), x, c)
    down_k = at_bulk(lax.rem(k + 3, 4), x, c)
    up_x = at_bulk(k, lax.rem(x + 1, 4), c)
    down_x = at_bulk(k, lax.rem(x + 3, 4), c)
    far_x = at_bulk(k, lax.rem(x + 2, 4), c)
    up_y = (zl * 8 + lax.rem(y + 1, 8), bulk)
    down_y = (zl * 8 + lax.rem(y + 7, 8), bulk)
    sibling = at_bulk(k, x, 1 - c)

    stage_me = (low, y, z)
    stage_peer = (
        lambda j: (lang, k * 8 + lax.rem(low + j, 8)),
        lambda j: (zl * 8 + lax.rem(y + j, 8), bulk),
        lambda j: (lax.rem(z + j, 2) * 8 + y, (lax.rem(z + j, 8) // 2) * 8 + low),
    )

    barrier = pltpu.get_barrier_semaphore()
    for stage in range(3):
        for j in range(1, 8):
            pl.semaphore_signal(
                barrier, inc=1, device_id=stage_peer[stage](j), device_id_type=MESH
            )

    own = held.at[bulk]
    own_load = pltpu.make_async_copy(targets_hbm, own, small_sem.at[0])
    ids_load = pltpu.make_async_copy(ids_hbm, ids, small_sem.at[1])
    centers_load = pltpu.make_async_copy(centers_hbm, centers, small_sem.at[2])
    own_load.start()
    ids_load.start()
    centers_load.start()
    loads = []
    for b in range(nblk):
        load = pltpu.make_async_copy(
            sources_hbm.at[pl.ds(b * rowblk, rowblk), :], raw.at[b], load_sem.at[b]
        )
        load.start()
        loads.append(load)

    own_load.wait()
    pl.semaphore_wait(barrier, 21)

    started = []

    def send(ref, send_sem, recv_sem, device):
        copy = pltpu.make_async_remote_copy(
            src_ref=ref, dst_ref=ref, send_sem=send_sem, recv_sem=recv_sem,
            device_id=device, device_id_type=MESH,
        )
        copy.start()
        started.append(copy)

    def arrived(ref, send_sem, recv_sem):
        pltpu.make_async_remote_copy(
            src_ref=ref, dst_ref=ref, send_sem=send_sem, recv_sem=recv_sem,
            device_id=sibling, device_id_type=MESH,
        ).wait_recv()

    def rows(dk, dx, which, cc=c):
        return held.at[slot(dk, dx, cc), pl.ds(pl.multiple_of(which * half, half), half), :]

    def lanes(dk, dx, which, side):
        return held.at[
            slot(dk, dx, cc=c),
            pl.ds(pl.multiple_of(which * half, half), half),
            pl.ds(side * (width // 2), width // 2),
        ]

    def share(dk, dx):
        ref = rows(dk, dx, mine)
        send(
            ref, y_send.at[dk, dx], y_recv.at[dk, dx],
            up_y if (dk + dx) % 2 == 0 else down_y,
        )
        send(ref, c_send.at[0, dk, dx], c_recv.at[0, dk, dx], sibling)

    def along_x(dk):
        ref = rows(dk, 0, mine)
        send(ref, x_send.at[dk, 0], x_recv.at[dk, 0], up_x)
        send(ref, x_send.at[dk, 1], x_recv.at[dk, 1], down_x)
        if dk in FAR_DIRECT:
            send(ref, x_send.at[dk, 2], x_recv.at[dk, 2], far_x)

    def relay_x(dk):
        arrived(rows(dk, 3, mine), x_send.at[dk, 0], x_recv.at[dk, 0])
        if dk not in FAR_DIRECT:
            send(lanes(dk, 3, mine, 0), x_send.at[dk, 2], x_recv.at[dk, 2], up_x)
        share(dk, 3)
        arrived(rows(dk, 1, mine), x_send.at[dk, 1], x_recv.at[dk, 1])
        if dk not in FAR_DIRECT:
            send(lanes(dk, 1, mine, 1), x_send.at[dk, 3], x_recv.at[dk, 3], down_x)
        share(dk, 1)

    def finish_x(dk):
        if dk in FAR_DIRECT:
            arrived(rows(dk, 2, mine), x_send.at[dk, 2], x_recv.at[dk, 2])
        else:
            arrived(lanes(dk, 2, mine, 0), x_send.at[dk, 2], x_recv.at[dk, 2])
            arrived(lanes(dk, 2, mine, 1), x_send.at[dk, 3], x_recv.at[dk, 3])
        share(dk, 2)

    def from_y(dk, dxs=(0, 3, 1, 2)):
        for dx in dxs:
            if (dk, dx) == (0, 0):
                continue
            ref = rows(dk, dx, 1 - mine)
            arrived(ref, y_send.at[dk, dx], y_recv.at[dk, dx])
            send(ref, c_send.at[1, dk, dx], c_recv.at[1, dk, dx], sibling)

    def from_sibling(dk):
        for dx in range(4):
            if (dk, dx) == (0, 0):
                arrived(held.at[slot(0, 0, 1 - c)], c_send.at[0, 0, 0], c_recv.at[0, 0, 0])
                continue
            arrived(rows(dk, dx, mine, 1 - c), c_send.at[0, dk, dx], c_recv.at[0, dk, dx])
            arrived(rows(dk, dx, 1 - mine, 1 - c), c_send.at[1, dk, dx], c_recv.at[1, dk, dx])

    def score(dk):
        first = lax.rem(k + dk, 4) * 8

        def score_step(b, carried):
            peak, weight = carried
            tile = lax.dot_general(
                centered[b], held[pl.ds(first, 8)].reshape(group, width),
                (((1,), (1,)), ((), ())), preferred_element_type=jnp.float32,
            ) * temper
            scores[dk, b] = tile
            grouped = tile.reshape(tile.shape[0] // 8, 8, group)
            new_peak = jnp.maximum(peak, jnp.max(grouped, axis=0))
            weight = weight * jnp.exp(peak - new_peak) + jnp.sum(
                jnp.exp(grouped - new_peak[None]), axis=0
            )
            return new_peak, weight

        peak, weight = lax.fori_loop(
            0, nblk, score_step,
            (jnp.full((8, group), -jnp.inf, jnp.float32), jnp.zeros((8, group), jnp.float32)),
        )
        top = jnp.max(peak, axis=0, keepdims=True)
        hub = top + jnp.log(jnp.sum(weight * jnp.exp(peak - top), axis=0, keepdims=True))
        for j in range(group // 128):
            hubs[0, pl.ds(lax.rem(k + dk, 4) * (group // 128) + j, 1), :] = hub[
                :, j * 128:(j + 1) * 128
            ]

    send(rows(0, 0, mine), z_send.at[0], z_recv.at[0], up_k)
    send(rows(0, 0, mine), z_send.at[1], z_recv.at[1], down_k)
    along_x(0)
    send(own, c_send.at[0, 0, 0], c_recv.at[0, 0, 0], sibling)

    ids_load.wait()
    centers_load.wait()
    for b in range(nblk):
        loads[b].wait()
        offset = centers[pl.ds(ids[b], 1), :]
        centered[b] = (raw[b].astype(jnp.float32) - offset).astype(jnp.bfloat16)

    relay_x(0)
    arrived(rows(3, 0, mine), z_send.at[0], z_recv.at[0])
    send(lanes(3, 0, mine, 0), z_send.at[2], z_recv.at[2], up_k)
    along_x(3)
    share(3, 0)
    arrived(rows(1, 0, mine), z_send.at[1], z_recv.at[1])
    send(lanes(1, 0, mine, 1), z_send.at[3], z_recv.at[3], down_k)
    along_x(1)
    share(1, 0)
    finish_x(0)
    relay_x(3)
    relay_x(1)
    from_y(0)
    arrived(lanes(2, 0, mine, 0), z_send.at[2], z_recv.at[2])
    arrived(lanes(2, 0, mine, 1), z_send.at[3], z_recv.at[3])
    along_x(2)
    share(2, 0)
    finish_x(3)
    finish_x(1)
    from_sibling(0)
    score(0)
    relay_x(2)
    from_y(3)
    from_y(1)
    finish_x(2)
    from_sibling(3)
    score(3)
    from_y(2)
    from_sibling(1)
    score(1)
    from_sibling(2)
    score(2)

    for stage in range(3):
        me = stage_me[stage]
        for j in SENDS:
            copy = pltpu.make_async_remote_copy(
                src_ref=hubs.at[stage], dst_ref=parts.at[stage, me],
                send_sem=r_send.at[stage, j], recv_sem=r_recv.at[stage, j],
                device_id=stage_peer[stage](j), device_id_type=MESH,
            )
            copy.start()
            started.append(copy)
        parts[stage, me] = hubs[stage]
        for j in range(1, 8):
            arrived(
                parts.at[stage, lax.rem(me + 8 - j, 8)], r_send.at[stage, j], r_recv.at[stage, j]
            )
        every = parts[stage]
        most = jnp.max(every, axis=0)
        hubs[stage + 1] = most + jnp.log(jnp.sum(jnp.exp(every - most[None]), axis=0))

    line = hubs[3, pl.ds(bulk // 4, 1), :]
    quarter = bulk % 4
    own_hub = jnp.zeros((1, piece_rows), jnp.float32)
    for q in range(4):
        own_hub = jnp.where(quarter == q, line[:, q * piece_rows:(q + 1) * piece_rows], own_hub)
    hub_ref[...] = own_hub

    hub_rows = [
        jnp.concatenate(
            [
                hubs[3, pl.ds(lax.rem(k + dk, 4) * (group // 128) + j, 1), :]
                for j in range(group // 128)
            ],
            axis=1,
        )
        for dk in range(4)
    ]
    eye = lax.broadcasted_iota(jnp.int32, (rowblk, rowblk), 0) == lax.broadcasted_iota(
        jnp.int32, (rowblk, rowblk), 1
    )

    def read_step(b, unused):
        tiles = [scores[dk, b] for dk in range(4)]
        adjusted = [2.0 * tiles[dk] - hub_rows[dk] for dk in range(4)]
        most = functools.reduce(jnp.maximum, adjusted)
        most = jnp.max(most, axis=1, keepdims=True)
        weights = [jnp.exp(adjusted[dk] - most) for dk in range(4)]
        summed = jnp.sum(sum(weights), axis=1, keepdims=True)
        matched = jnp.sum(
            sum(weights[dk] * tiles[dk] for dk in range(4)), axis=1, keepdims=True
        )
        logsum = most + jnp.log(summed)
        match = matched / summed
        logsum_ref[pl.ds(b, 1), :] = jnp.sum(jnp.where(eye, logsum, 0.0), axis=0, keepdims=True)
        match_ref[pl.ds(b, 1), :] = jnp.sum(jnp.where(eye, match, 0.0), axis=0, keepdims=True)
        return unused

    lax.fori_loop(0, nblk, read_step, 0)
    for copy in started:
        copy.wait_send()


def hand_out(hub_in, logsum_in, match_in, hub_out, logsum_out, match_out, sems):
    copies = [
        pltpu.make_async_copy(src, dst, sems.at[i])
        for i, (src, dst) in enumerate(
            ((hub_in, hub_out), (logsum_in, logsum_out), (match_in, match_out))
        )
    ]
    for copy in copies:
        copy.start()
    for copy in copies:
        copy.wait()


def per_device(sources, lang_ids, centers, targets):
    rows, width = sources.shape
    nblk = lang_ids.shape[0]
    rowblk = rows // nblk
    piece_rows = targets.shape[0]
    count = 32 * piece_rows
    vmem = pl.BlockSpec(memory_space=pltpu.VMEM)
    dma = pltpu.SemaphoreType.DMA
    hub, logsum, match = pl.pallas_call(
        functools.partial(kernel, rowblk),
        out_shape=(
            jax.ShapeDtypeStruct((1, piece_rows), jnp.float32),
            jax.ShapeDtypeStruct((nblk, rowblk), jnp.float32),
            jax.ShapeDtypeStruct((nblk, rowblk), jnp.float32),
        ),
        in_specs=[pl.BlockSpec(memory_space=pltpu.HBM)] * 4,
        out_specs=(vmem, vmem, vmem),
        scratch_shapes=[
            pltpu.SMEM((nblk,), jnp.int32),
            pltpu.VMEM(centers.shape, jnp.float32),
            pltpu.VMEM((nblk, rowblk, width), jnp.bfloat16),
            pltpu.VMEM((nblk, rowblk, width), jnp.bfloat16),
            pltpu.VMEM((32, piece_rows, width), jnp.bfloat16),
            pltpu.VMEM((4, nblk, rowblk, count // 4), jnp.float32),
            pltpu.VMEM((4, 8, count // 8), jnp.float32),
            pltpu.VMEM((3, 8, 8, count // 8), jnp.float32),
            dma((nblk,)), dma((3,)),
            dma((4,)), dma((4,)),
            dma((4, 4)), dma((4, 4)),
            dma((4, 4)), dma((4, 4)),
            dma((2, 4, 4)), dma((2, 4, 4)),
            dma((3, 8)), dma((3, 8)),
        ],
        compiler_params=pltpu.CompilerParams(
            collective_id=0, has_side_effects=True, vmem_limit_bytes=67043328
        ),
        name="csls",
    )(lang_ids, centers, targets, sources)
    hub, logsum, match = pl.pallas_call(
        hand_out,
        out_shape=tuple(jax.ShapeDtypeStruct(a.shape, a.dtype) for a in (hub, logsum, match)),
        in_specs=[pl.BlockSpec(memory_space=pl.ANY)] * 3,
        out_specs=[pl.BlockSpec(memory_space=pltpu.VMEM)] * 3,
        scratch_shapes=[dma((3,))],
        name="hand_out",
    )(hub, logsum, match)
    return hub.reshape(piece_rows), logsum.reshape(rows), match.reshape(rows)


def solution(mesh):
    in_specs = (P(("lang", "bulk"), None), P(("lang", "bulk")), P(), P("bulk", None))
    out_specs = (P("bulk"), P(("lang", "bulk")), P(("lang", "bulk")))
    return jax.shard_map(
        per_device, mesh=mesh, in_specs=in_specs, out_specs=out_specs, check_vma=False
    )
```

time: 63.7 us -> 55.8 us (0.88)
  local copies, waits for them, and re-layouts: 5.62 us -> 0 us
  Pallas kernels: 57.1 us -> 55 us
    unnamed x11 -> x0, local copies, waits for them, and re-layouts: 5.62 us -> none
    pallas_call x1, Pallas kernels: 57.1 us -> 53.7 us  [per_device(): pl.pallas_call(functools.partial(kernel, rowblk), out_shape=(jax.ShapeDty...]
    pallas_call x0 -> x1, Pallas kernels: none -> 1.32 us  [per_device(): pl.pallas_call(hand_out, out_shape=tuple((jax.ShapeDtypeStruct(a.shape, a...]
where the time goes in v2:
time: 55.8 us; the launch traced here: 55.6 us
  Pallas kernels  55 us (99%)
  between operations  0.64 us (1%)
    pallas_call x1, Pallas kernels, per_device(): pl.pallas_call(functools.partial(kernel, rowblk), out_shape=(jax.ShapeDty...  53.7 us
    pallas_call x1, Pallas kernels, per_device(): pl.pallas_call(hand_out, out_shape=tuple((jax.ShapeDtypeStruct(a.shape, a...  1.32 us

profile of v2, /device:TPU:1, one launch (start us, length us, event | category | flops | bytes accessed | tf_op | source)
XLA Modules:
  0.0 55.6 jit_solution(15289006098652960375)
XLA Ops:
  0.6 53.7 %csls.1 = (f32[1,32]{1,0:T(1,128)}, f32[8,128]{1,0:T(8,128)}, f32[8,128]{1,0:T(8,128)}) custom-call(s32[8]{0:T(128)} %ids_hbm.1, f32[16,1024]{1,0:T(8,128)} %centers_hbm.1, bf16[32,1024]{1,0:T(8,128)(2,1)} %targets_hbm.1, bf16[1024,1024]{1,0:T(8,128)(2,1)} %sources_hbm.1), custom_call_target="tpu_custom_call" | custom-call | tf_op jit(solution)/shard_map/csls/pallas_call | solution.py:314
  54.3 1.3 %hand_out.1 = (f32[1,32]{1,0:T(1,128)}, f32[8,128]{1,0:T(8,128)}, f32[8,128]{1,0:T(8,128)}) custom-call(f32[1,32]{1,0:T(1,128)} %get-tuple-element.9.hub_in, f32[8,128]{1,0:T(8,128)} %get-tuple-element.10.logsum_in, f32[8,128]{1,0:T(8,128)} %get-tuple-element.11.match_in), custom_call_target="tpu_custom_call" | custom-call | tf_op jit(solution)/shard_map/hand_out/pallas_call | solution.py:344

commit v3 on v2

--- a/solution.py
+++ b/solution.py
@@ -10,6 +10,7 @@
 MESH = pl.DeviceIdType.MESH
 SENDS = (4, 3, 5, 2, 6, 1, 7)
 FAR_DIRECT = (0, 1, 2, 3)
+SPAN = 4
 
 
 def kernel(
@@ -162,10 +163,11 @@
         def score_step(b, carried):
             peak, weight = carried
             tile = lax.dot_general(
-                centered[b], held[pl.ds(first, 8)].reshape(group, width),
+                centered[pl.ds(b * SPAN, SPAN)].reshape(SPAN * rowblk, width),
+                held[pl.ds(first, 8)].reshape(group, width),
                 (((1,), (1,)), ((), ())), preferred_element_type=jnp.float32,
             ) * temper
-            scores[dk, b] = tile
+            scores[dk, pl.ds(b * SPAN, SPAN)] = tile.reshape(SPAN, rowblk, group)
             grouped = tile.reshape(tile.shape[0] // 8, 8, group)
             new_peak = jnp.maximum(peak, jnp.max(grouped, axis=0))
             weight = weight * jnp.exp(peak - new_peak) + jnp.sum(
@@ -174,7 +176,7 @@
             return new_peak, weight
 
         peak, weight = lax.fori_loop(
-            0, nblk, score_step,
+            0, nblk // SPAN, score_step,
             (jnp.full((8, group), -jnp.inf, jnp.float32), jnp.zeros((8, group), jnp.float32)),
         )
         top = jnp.max(peak, axis=0, keepdims=True)

time: 55.8 us -> 52.6 us (0.943)
  Pallas kernels: 55 us -> 51.5 us
    pallas_call x1, Pallas kernels: 53.7 us -> 50.2 us  [per_device(): pl.pallas_call(functools.partial(kernel, rowblk), out_shape=(jax.ShapeDty...]
where the time goes in v3:
time: 52.6 us; the launch traced here: 52.1 us
  Pallas kernels  51.5 us (98%)
  between operations  0.64 us (1%)
    pallas_call x1, Pallas kernels, per_device(): pl.pallas_call(functools.partial(kernel, rowblk), out_shape=(jax.ShapeDty...  50.2 us
    pallas_call x1, Pallas kernels, per_device(): pl.pallas_call(hand_out, out_shape=tuple((jax.ShapeDtypeStruct(a.shape, a...  1.32 us

profile of v3, /device:TPU:1, one launch (start us, length us, event | category | flops | bytes accessed | tf_op | source)
XLA Modules:
  0.0 52.1 jit_solution(3287860335175066)
XLA Ops:
  0.6 50.2 %csls.1 = (f32[1,32]{1,0:T(1,128)}, f32[8,128]{1,0:T(8,128)}, f32[8,128]{1,0:T(8,128)}) custom-call(s32[8]{0:T(128)} %ids_hbm.1, f32[16,1024]{1,0:T(8,128)} %centers_hbm.1, bf16[32,1024]{1,0:T(8,128)(2,1)} %targets_hbm.1, bf16[1024,1024]{1,0:T(8,128)(2,1)} %sources_hbm.1), custom_call_target="tpu_custom_call" | custom-call | tf_op jit(solution)/shard_map/csls/pallas_call | solution.py:316
  50.8 1.3 %hand_out.1 = (f32[1,32]{1,0:T(1,128)}, f32[8,128]{1,0:T(8,128)}, f32[8,128]{1,0:T(8,128)}) custom-call(f32[1,32]{1,0:T(1,128)} %get-tuple-element.9.hub_in, f32[8,128]{1,0:T(8,128)} %get-tuple-element.10.logsum_in, f32[8,128]{1,0:T(8,128)} %get-tuple-element.11.match_in), custom_call_target="tpu_custom_call" | custom-call | tf_op jit(solution)/shard_map/hand_out/pallas_call | solution.py:346

commit v4 on v3

--- a/solution.py
+++ b/solution.py
@@ -287,7 +287,7 @@
         match_ref[pl.ds(b, 1), :] = jnp.sum(jnp.where(eye, match, 0.0), axis=0, keepdims=True)
         return unused
 
-    lax.fori_loop(0, nblk, read_step, 0)
+    lax.fori_loop(0, nblk, read_step, 0, unroll=2)
     for copy in started:
         copy.wait_send()
 

time: 52.6 us -> 52.1 us (level)
  Pallas kernels: 51.5 us -> 50.9 us
    pallas_call x1, Pallas kernels: 50.2 us -> 49.6 us  [per_device(): pl.pallas_call(functools.partial(kernel, rowblk), out_shape=(jax.ShapeDty...]
where the time goes in v4:
time: 52.1 us; the launch traced here: 51.5 us
  Pallas kernels  50.9 us (98%)
  between operations  0.64 us (1%)
    pallas_call x1, Pallas kernels, per_device(): pl.pallas_call(functools.partial(kernel, rowblk), out_shape=(jax.ShapeDty...  49.6 us
    pallas_call x1, Pallas kernels, per_device(): pl.pallas_call(hand_out, out_shape=tuple((jax.ShapeDtypeStruct(a.shape, a...  1.32 us

profile of v4, /device:TPU:1, one launch (start us, length us, event | category | flops | bytes accessed | tf_op | source)
XLA Modules:
  0.0 51.5 jit_solution(3397820498852747695)
XLA Ops:
  0.6 49.6 %csls.1 = (f32[1,32]{1,0:T(1,128)}, f32[8,128]{1,0:T(8,128)}, f32[8,128]{1,0:T(8,128)}) custom-call(s32[8]{0:T(128)} %ids_hbm.1, f32[16,1024]{1,0:T(8,128)} %centers_hbm.1, bf16[32,1024]{1,0:T(8,128)(2,1)} %targets_hbm.1, bf16[1024,1024]{1,0:T(8,128)(2,1)} %sources_hbm.1), custom_call_target="tpu_custom_call" | custom-call | tf_op jit(solution)/shard_map/csls/pallas_call | solution.py:316
  50.2 1.3 %hand_out.1 = (f32[1,32]{1,0:T(1,128)}, f32[8,128]{1,0:T(8,128)}, f32[8,128]{1,0:T(8,128)}) custom-call(f32[1,32]{1,0:T(1,128)} %get-tuple-element.9.hub_in, f32[8,128]{1,0:T(8,128)} %get-tuple-element.10.logsum_in, f32[8,128]{1,0:T(8,128)} %get-tuple-element.11.match_in), custom_call_target="tpu_custom_call" | custom-call | tf_op jit(solution)/shard_map/hand_out/pallas_call | solution.py:346
